TPU v7x, 32 devices: a whole 2x2x4 slice. The times are simulated.
32 devices in a mesh: occ: 16 (over z, y, core), vir: 2 (over x).
Axes of the slice: x: 2, y: 2, z: 4, core: 2. Of those that a mesh axis runs over, the one named last changes fastest.
Arguments:
- lambda_triples: bfloat16 [256, 320, 320], P('occ', 'vir'), may hold values from -6 to 6
- amplitude_triples: bfloat16 [256, 320, 320], P('occ', 'vir'), may hold values from -6 to 6
- spin_extent: int32 [256], P('occ'), may hold values from 80 to 320
- ladder_weight: bfloat16 [320, 320], P(None, 'vir'), may hold values from -0.3125 to 0.3125
- cycle_weight: bfloat16 [320, 40], replicated, may hold values from -0.3125 to 0.3125
- lambda_doubles: bfloat16 [40, 320], P(None, 'vir'), may hold values from -1 to 1
Outputs:
- residual: bfloat16 [256, 320, 320], P('occ', 'vir')
All inputs are finite; a program needn't handle non-finite values.
Results may differ from a plain program's by a relative error of at most 0.0043.
Values may be sent and summed in bfloat16 or wider, within the bound.
No kernel may reach another device: no remote copies, remote signals or barrier semaphores. Data moves between devices by JAX's collectives and lax.ppermute only.
A program may use at most 64 MiB of HBM per device.

v0:
```python
import jax
import jax.numpy as jnp
from jax import lax
from jax.sharding import PartitionSpec as P


def on_device(
    lambda_triples, amplitude_triples, spin_extent, ladder_weight, cycle_weight, lambda_doubles
):
    f32 = jnp.float32
    width = lambda_triples.shape[2]
    triples_all = lambda_triples.shape[0] * lax.axis_size("occ")
    columns = jnp.arange(width, dtype=jnp.int32)
    keep = columns[None, :] < spin_extent[:, None]
    masked = jnp.where(keep[:, None, :], lambda_triples, jnp.zeros_like(lambda_triples))
    ladder_full, doubles_full = (
        lax.all_gather(ladder_weight, "vir", axis=1, tiled=True),
        lax.all_gather(lambda_doubles, "vir", axis=1, tiled=True),
    )
    ladder_term = jnp.einsum("tae,eb->tab", masked, ladder_full, preferred_element_type=f32)
    cycle_mid = jnp.einsum(
        "tae,em->tam", amplitude_triples, cycle_weight, preferred_element_type=f32
    ).astype(jnp.bfloat16)
    cycle_term = jnp.einsum("tam,mb->tab", cycle_mid, doubles_full, preferred_element_type=f32)
    partial_density = jnp.einsum(
        "tae,tbe->ab",
        masked,
        lax.all_gather(amplitude_triples, "vir", axis=1, tiled=True),
        preferred_element_type=f32,
    )
    density = lax.psum(partial_density, "occ")
    density = (density / jnp.sqrt(f32(triples_all * width))).astype(jnp.bfloat16)
    density_term = jnp.einsum(
        "ac,tcb->tab",
        density,
        lax.all_gather(masked, "vir", axis=1, tiled=True),
        preferred_element_type=f32,
    )
    density_term = density_term / jnp.sqrt(f32(width))
    return (ladder_term + cycle_term + density_term).astype(jnp.bfloat16)


def solution(mesh):
    return jax.shard_map(
        on_device,
        mesh=mesh,
        in_specs=(
            P("occ", "vir", None),
            P("occ", "vir", None),
            P("occ"),
            P(None, "vir"),
            P(),
            P(None, "vir"),
        ),
        out_specs=P("occ", "vir", None),
        check_vma=False,
    )
```

profile of v0, /device:TPU:8, one launch (start us, length us, event | category | flops | bytes accessed | tf_op | source)
XLA Modules:
  0.0 227.4 jit_solution(11360172198900712387)
XLA Ops:
  6.5 0.0 copy-start
  6.5 0.0 copy-start.3
  6.5 0.0 copy-start.2
  6.5 0.0 all-gather.6.cloned.1.call-start
  6.5 0.7 all-gather.6.cloned.1.call-update
  7.3 0.0 all-gather.4.cloned.1.call-start
  7.3 0.7 iota_compare_fusion
  8.0 3.0 %broadcast_select_fusion = bf16[16,160,320]{2,1,0:T(8,128)(2,1)} fusion(bf16[16,160,320]{2,1,0:T(8,128)(2,1)} %param.6, pred[16,320]{1,0:T(8,128)(4,1)S(1)} %iota_compare_fusion), kind=kLoop, calls=%fused_computation.2 | loop fusion | flops 819200 | bytes 3281920 | tf_op jit(solution)/shard_map/jit(_where)/select_n | solution.py:15
  11.1 0.0 copy-start.1
  11.1 0.0 all-gather.4.cloned.1.call-update
  11.1 0.0 all-reduce.2.cloned.1.call-start
  11.2 0.0 copy-done.3
  11.2 4.6 %all-gather = bf16[2,160,40]{1,2,0:T(8,128)(2,1)S(1)} all-gather(bf16[1,160,40]{1,2,0:T(8,128)(2,1)S(1)} %bitcast.27), channel_id=1, replica_groups=mesh['occ'=16,'vir'=2] {'vir'}, dimensions={0}, use_global_device_ids=true | all-gather | bytes 38400 | tf_op jit(solution)/shard_map/all_gather | solution.py:18
  15.8 0.1 reshape.21
  15.9 0.0 copy-done.2
  15.9 6.4 %all_gather.12 = bf16[320,320]{0,1:T(8,128)(2,1)S(1)} all-gather(bf16[320,160]{0,1:T(8,128)(2,1)S(1)} %copy-done.2), channel_id=1, replica_groups=mesh['occ'=16,'vir'=2] {'vir'}, dimensions={1}, use_global_device_ids=true | all-gather | bytes 307200 | tf_op jit(solution)/shard_map/all_gather | solution.py:17
  22.3 4.9 %fusion.2 = f32[16,160,320]{2,1,0:T(8,128)} fusion(bf16[16,160,320]{2,1,0:T(8,128)(2,1)} %broadcast_select_fusion, bf16[320,320]{0,1:T(8,128)(2,1)S(1)} %all_gather.12), kind=kOutput, calls=%fused_computation.6 | convolution fusion | flops 524288000 | bytes 5120000 | tf_op jit(solution)/shard_map/tae,eb->tab/dot_general | solution.py:20
  27.2 36.7 %all-gather.6.cloned.1.call-done = bf16[16,320,320]{2,1,0:T(8,128)(2,1)} async-done(((bf16[16,160,320]{2,1,0:T(8,128)(2,1)}), bf16[16,320,320]{2,1,0:T(8,128)(2,1)}) %all-gather.6.cloned.1.call-update) | async-done | bytes 3276816 | tf_op jit(solution)/shard_map/all_gather | solution.py:28
  63.9 0.0 copy-done.1
  63.9 4.4 %convolution_bitcast_fusion = f32[160,320]{1,0:T(8,128)} fusion(bf16[16,160,320]{2,1,0:T(8,128)(2,1)S(1)} %copy-done.1, bf16[16,320,320]{2,1,0:T(8,128)(2,1)} %all-gather.6.cloned.1.call-done), kind=kOutput, calls=%fused_computation.5 | convolution fusion | flops 524288000 | bytes 5120000 | tf_op jit(solution)/shard_map/tae,tbe->ab/dot_general | solution.py:25
  68.3 0.0 all-reduce.2.cloned.1.call-update
  68.3 0.0 copy-done
  68.3 5.2 %fusion.1 = f32[16,160,320]{2,1,0:T(8,128)} fusion(bf16[320,40,1]{0,1,2:T(8,128)(2,1)S(1)} %reshape.21, bf16[16,160,320]{2,1,0:T(8,128)(2,1)} %param.7, bf16[320,40]{0,1:T(8,128)(2,1)S(1)} %copy-done), kind=kOutput, calls=%fused_computation.4 | convolution fusion | flops 131174400 | bytes 4966400 | tf_op jit(solution)/shard_map/tam,mb->tab/dot_general | solution.py:24
  73.5 46.9 %all-gather.4.cloned.1.call-done = bf16[16,320,320]{2,1,0:T(8,128)(2,1)} async-done(((bf16[16,160,320]{2,1,0:T(8,128)(2,1)}), bf16[16,320,320]{2,1,0:T(8,128)(2,1)}) %all-gather.4.cloned.1.call-update) | async-done | bytes 3276816 | tf_op jit(solution)/shard_map/all_gather | solution.py:36
  120.4 93.5 %all-reduce.2.cloned.1.call-done = f32[160,320]{1,0:T(8,128)} async-done(((f32[160,320]{1,0:T(8,128)}), f32[160,320]{1,0:T(8,128)}) %all-reduce.2.cloned.1.call-update) | async-done | bytes 204816 | tf_op jit(solution)/shard_map/psum | solution.py:31
  213.9 7.0 %fusion = bf16[16,160,320]{2,1,0:T(8,128)(2,1)} fusion(f32[16,160,320]{2,1,0:T(8,128)} %fusion.2, f32[16,160,320]{2,1,0:T(8,128)} %fusion.1, bf16[16,320,320]{2,1,0:T(8,128)(2,1)} %all-gather.4.cloned.1.call-done, f32[160,320]{1,0:T(8,128)} %all-reduce.2.cloned.1.call-done), kind=kOutput, calls=%fused_computation.1 | convolution fusion | flops 527667200 | bytes 11673600 | tf_op jit(solution)/shard_map/ac,tcb->tab/dot_general | solution.py:33
  (1 shorter events, 0.0 us)
Async XLA Ops:
  6.5 61.8 %copy-start = (bf16[320,40]{0,1:T(8,128)(2,1)S(1)}, bf16[320,40]{0,1:T(8,128)(2,1)}, u32[]{:S(2)}) copy-start(bf16[320,40]{0,1:T(8,128)(2,1)} %param.10) | copy-start | bytes 76804
  6.5 4.6 %copy-start.3 = (bf16[40,160]{1,0:T(8,128)(2,1)S(1)}, bf16[40,160]{1,0:T(8,128)(2,1)}, u32[]{:S(2)}) copy-start(bf16[40,160]{1,0:T(8,128)(2,1)} %param.11) | copy-start | bytes 38404
  6.5 9.4 %copy-start.2 = (bf16[320,160]{0,1:T(8,128)(2,1)S(1)}, bf16[320,160]{0,1:T(8,128)(2,1)}, u32[]{:S(2)}) copy-start(bf16[320,160]{0,1:T(8,128)(2,1)} %param.9) | copy-start | bytes 307204
  6.5 57.4 %all-gather.6.cloned.1.call-start = ((), (), s32[]{:S(2)}) async-start(), calls=%async_computation.1 | async-start | bytes 5898240 | tf_op jit(solution)/shard_map/all_gather | solution.py:28
  7.3 113.1 %all-gather.4.cloned.1.call-start = ((), (), s32[]{:S(2)}) async-start(), calls=%async_computation | async-start | bytes 5898240 | tf_op jit(solution)/shard_map/all_gather | solution.py:36
  11.1 52.8 %copy-start.1 = (bf16[16,160,320]{2,1,0:T(8,128)(2,1)S(1)}, bf16[16,160,320]{2,1,0:T(8,128)(2,1)}, u32[]{:S(2)}) copy-start(bf16[16,160,320]{2,1,0:T(8,128)(2,1)} %broadcast_select_fusion) | copy-start | bytes 4915204
  11.1 202.8 %all-reduce.2.cloned.1.call-start = ((), (), s32[]{:S(2)}) async-start(), calls=%async_computation.2 | async-start | bytes 491520 | tf_op jit(solution)/shard_map/psum | solution.py:31
Sparse Core Ops, SparseCore 0:
  8.9 54.9 all-gather.5
  65.4 54.8 all-gather.3
  123.8 90.0 all-reduce.1
where the time goes:
time: 228 us; the launch traced here: 227 us
  waiting for transfers between devices  178 us (78%)
  matrix products  21.4 us (9%)
  between operations  13.1 us (6%)
  blocking collectives  11 us (5%)
  other arithmetic  3.77 us (2%)
    psum x1, waiting for transfers between devices, on_device(): density = lax.psum(partial_density, 'occ')  93.5 us
    all_gather x1, waiting for transfers between devices, on_device(): lax.all_gather(masked, 'vir', axis=1, tiled=True)  46.9 us
    all_gather x1, waiting for transfers between devices, on_device(): lax.all_gather(amplitude_triples, 'vir', axis=1, tiled=True)  36.7 us
    dot_general x1, matrix products, on_device(): jnp.einsum('ac,tcb->tab', density, lax.all_gather(masked, 'vir', axis=1,...  6.97 us
    all_gather x1, blocking collectives, on_device(): lax.all_gather(ladder_weight, 'vir', axis=1, tiled=True)  6.43 us
    dot_general x1, matrix products, on_device(): jnp.einsum('tam,mb->tab', cycle_mid, doubles_full, preferred_element_type...  5.16 us
    dot_general x1, matrix products, on_device(): jnp.einsum('tae,eb->tab', masked, ladder_full, preferred_element_type=f32)  4.91 us
    all_gather x1, blocking collectives, on_device(): lax.all_gather(lambda_doubles, 'vir', axis=1, tiled=True)  4.59 us
  transfers between devices with their start and end apart: 3, of which 3 were waited for; matrix products, arithmetic and copies ran while one was open for 8% of the time, Pallas kernels for 0%

commit v1 on v0

--- a/solution.py
+++ b/solution.py
@@ -28,7 +28,9 @@
         lax.all_gather(amplitude_triples, "vir", axis=1, tiled=True),
         preferred_element_type=f32,
     )
-    density = lax.psum(partial_density, "occ")
+    density = partial_density
+    for hop in (1, 2, 4, 8):
+        density = density + lax.ppermute(density, "occ", [(dev, dev ^ hop) for dev in range(16)])
     density = (density / jnp.sqrt(f32(triples_all * width))).astype(jnp.bfloat16)
     density_term = jnp.einsum(
         "ac,tcb->tab",

time: 228 us -> 137 us (0.60)
  waiting for transfers between devices: 178 us -> 80.6 us
  starting transfers between devices: 0.08 us -> 4.74 us
    psum x1 -> x0, waiting for transfers between devices: 93.5 us -> none  [on_device(): density = lax.psum(partial_density, 'occ')]
    all_gather x1, waiting for transfers between devices: 46.9 us -> 23.2 us  [on_device(): lax.all_gather(masked, 'vir', axis=1, tiled=True)]
    all_gather x1, waiting for transfers between devices: 36.7 us -> 52.7 us  [on_device(): lax.all_gather(amplitude_triples, 'vir', axis=1, tiled=True)]
    ppermute x0 -> x4, starting transfers between devices: none -> 4.69 us  [on_device(): lax.ppermute(density, 'occ', [(dev, dev ^ hop) for dev in range(16)])]
    ppermute x0 -> x4, waiting for transfers between devices: none -> 3.92 us  [on_device(): lax.ppermute(density, 'occ', [(dev, dev ^ hop) for dev in range(16)])]
    all_gather x1, blocking collectives: 6.43 us -> 8.74 us  [on_device(): lax.all_gather(ladder_weight, 'vir', axis=1, tiled=True)]
  transfers between devices with their start and end apart: 3 -> 6, of which waited for: 3 -> 4; matrix products, arithmetic and copies ran while one was open for 8% -> 12% of each run, Pallas kernels for 0% -> 0%
where the time goes in v1:
time: 137 us; the launch traced here: 136 us
  waiting for transfers between devices  80.6 us (59%)
  matrix products  19.6 us (14%)
  between operations  13.5 us (10%)
  blocking collectives  13.2 us (10%)
  starting transfers between devices  4.74 us (3%)
  other arithmetic  3.85 us (3%)
    all_gather x1, waiting for transfers between devices, on_device(): lax.all_gather(amplitude_triples, 'vir', axis=1, tiled=True)  52.7 us
    all_gather x1, waiting for transfers between devices, on_device(): lax.all_gather(masked, 'vir', axis=1, tiled=True)  23.2 us
    all_gather x1, blocking collectives, on_device(): lax.all_gather(ladder_weight, 'vir', axis=1, tiled=True)  8.74 us
    dot_general x1, matrix products, on_device(): jnp.einsum('ac,tcb->tab', density, lax.all_gather(masked, 'vir', axis=1,...  6.91 us
    dot_general x1, matrix products, on_device(): jnp.einsum('tam,mb->tab', cycle_mid, doubles_full, preferred_element_type...  5.14 us
    ppermute x4, starting transfers between devices, on_device(): lax.ppermute(density, 'occ', [(dev, dev ^ hop) for dev in range(16)])  4.69 us
    all_gather x1, blocking collectives, on_device(): lax.all_gather(lambda_doubles, 'vir', axis=1, tiled=True)  4.45 us
    dot_general x1, matrix products, on_device(): jnp.einsum('tae,tbe->ab', masked, lax.all_gather(amplitude_triples, 'vir'...  4.32 us
  transfers between devices with their start and end apart: 6, of which 4 were waited for; matrix products, arithmetic and copies ran while one was open for 12% of the time, Pallas kernels for 0%

profile of v1, /device:TPU:8, one launch (start us, length us, event | category | flops | bytes accessed | tf_op | source)
XLA Modules:
  0.0 135.6 jit_solution(12270968385151010080)
XLA Ops:
  6.5 0.0 copy-start
  6.5 0.0 all-gather.6.cloned.1.call-start
  6.5 0.7 all-gather.6.cloned.1.call-update
  7.3 0.0 all-gather.4.cloned.1.call-start
  7.3 0.7 iota_compare_fusion
  8.0 3.0 %broadcast_select_fusion = bf16[16,160,320]{2,1,0:T(8,128)(2,1)} fusion(bf16[16,160,320]{2,1,0:T(8,128)(2,1)} %param.6, pred[16,320]{1,0:T(8,128)(4,1)S(1)} %iota_compare_fusion), kind=kLoop, calls=%fused_computation.2 | loop fusion | flops 819200 | bytes 3281920 | tf_op jit(solution)/shard_map/jit(_where)/select_n | solution.py:15
  11.1 0.0 all-gather.4.cloned.1.call-update
  11.1 0.0 copy-start.3
  11.1 0.0 copy-start.2
  11.1 0.0 copy-start.1
  11.1 52.7 %all-gather.6.cloned.1.call-done = bf16[16,320,320]{2,1,0:T(8,128)(2,1)} async-done(((bf16[16,160,320]{2,1,0:T(8,128)(2,1)}), bf16[16,320,320]{2,1,0:T(8,128)(2,1)}) %all-gather.6.cloned.1.call-update) | async-done | bytes 3276816 | tf_op jit(solution)/shard_map/all_gather | solution.py:28
  63.9 4.3 %convolution_bitcast_fusion = f32[160,320]{1,0:T(8,128)S(1)} fusion(bf16[16,160,320]{2,1,0:T(8,128)(2,1)} %broadcast_select_fusion, bf16[16,320,320]{2,1,0:T(8,128)(2,1)} %all-gather.6.cloned.1.call-done), kind=kOutput, calls=%fused_computation.5 | convolution fusion | flops 524288000 | bytes 5120000 | tf_op jit(solution)/shard_map/tae,tbe->ab/dot_general | solution.py:25
  68.2 0.1 collective-permute-start
  68.3 1.5 %collective-permute-done = f32[160,320]{1,0:T(8,128)S(1)} collective-permute-done((f32[160,320]{1,0:T(8,128)S(1)}, f32[160,320]{1,0:T(8,128)S(1)}, u32[]{:S(2)}, u32[]{:S(2)}) %collective-permute-start) | collective-permute-done | bytes 204832 | tf_op jit(solution)/shard_map/ppermute | solution.py:33
  69.8 1.5 %collective-permute-start.1 = (f32[160,320]{1,0:T(8,128)S(1)}, f32[160,320]{1,0:T(8,128)S(1)}, u32[]{:S(2)}, u32[]{:S(2)}) collective-permute-start(f32[160,320]{1,0:T(8,128)S(1)} %add.19), channel_id=1, source_target_pairs={{0,4},{2,6},{4,0},{6,2},{8,12},{10,14},{12,8},{14,10},{16,20},{18,... | collective-permute-start | bytes 614408 | tf_op jit(solution)/shard_map/ppermute | solution.py:33
  71.4 0.0 copy-done.3
  71.4 4.4 %all-gather = bf16[2,160,40]{1,2,0:T(8,128)(2,1)S(1)} all-gather(bf16[1,160,40]{1,2,0:T(8,128)(2,1)S(1)} %bitcast.27), channel_id=1, replica_groups=mesh['occ'=16,'vir'=2] {'vir'}, dimensions={0}, use_global_device_ids=true | all-gather | bytes 38400 | tf_op jit(solution)/shard_map/all_gather | solution.py:18
  75.8 0.1 reshape.21
  75.9 0.0 copy-done.2
  75.9 8.7 %all_gather.12 = bf16[320,320]{0,1:T(8,128)(2,1)S(1)} all-gather(bf16[320,160]{0,1:T(8,128)(2,1)S(1)} %copy-done.2), channel_id=1, replica_groups=mesh['occ'=16,'vir'=2] {'vir'}, dimensions={1}, use_global_device_ids=true | all-gather | bytes 307200 | tf_op jit(solution)/shard_map/all_gather | solution.py:17
  84.7 0.0 collective-permute-done.1
  84.7 0.6 collective-permute-start.2
  85.3 0.0 copy-done.1
  85.3 3.2 %fusion.2 = f32[16,160,320]{2,1,0:T(8,128)} fusion(bf16[16,160,320]{2,1,0:T(8,128)(2,1)S(1)} %copy-done.1, bf16[320,320]{0,1:T(8,128)(2,1)S(1)} %all_gather.12), kind=kOutput, calls=%fused_computation.6 | convolution fusion | flops 524288000 | bytes 5120000 | tf_op jit(solution)/shard_map/tae,eb->tab/dot_general | solution.py:20
  88.6 2.4 %collective-permute-done.2 = f32[160,320]{1,0:T(8,128)S(1)} collective-permute-done((f32[160,320]{1,0:T(8,128)S(1)}, f32[160,320]{1,0:T(8,128)S(1)}, u32[]{:S(2)}, u32[]{:S(2)}) %collective-permute-start.2) | collective-permute-done | bytes 204832 | tf_op jit(solution)/shard_map/ppermute | solution.py:33
  91.0 2.5 %collective-permute-start.3 = (f32[160,320]{1,0:T(8,128)S(1)}, f32[160,320]{1,0:T(8,128)S(1)}, u32[]{:S(2)}, u32[]{:S(2)}) collective-permute-start(f32[160,320]{1,0:T(8,128)S(1)} %add.21), channel_id=1, source_target_pairs={{0,16},{2,18},{4,20},{6,22},{8,24},{10,26},{12,28},{14,30},{16,0},... | collective-permute-start | bytes 614408 | tf_op jit(solution)/shard_map/ppermute | solution.py:33
  93.5 0.0 copy-done
  93.5 5.1 %fusion.1 = f32[16,160,320]{2,1,0:T(8,128)} fusion(bf16[320,40,1]{0,1,2:T(8,128)(2,1)S(1)} %reshape.21, bf16[16,160,320]{2,1,0:T(8,128)(2,1)} %param.7, bf16[320,40]{0,1:T(8,128)(2,1)S(1)} %copy-done), kind=kOutput, calls=%fused_computation.4 | convolution fusion | flops 131174400 | bytes 4966400 | tf_op jit(solution)/shard_map/tam,mb->tab/dot_general | solution.py:24
  98.6 23.2 %all-gather.4.cloned.1.call-done = bf16[16,320,320]{2,1,0:T(8,128)(2,1)} async-done(((bf16[16,160,320]{2,1,0:T(8,128)(2,1)}), bf16[16,320,320]{2,1,0:T(8,128)(2,1)}) %all-gather.4.cloned.1.call-update) | async-done | bytes 3276816 | tf_op jit(solution)/shard_map/all_gather | solution.py:38
  121.9 0.0 collective-permute-done.3
  121.9 6.9 %fusion = bf16[16,160,320]{2,1,0:T(8,128)(2,1)} fusion(f32[16,160,320]{2,1,0:T(8,128)} %fusion.2, f32[16,160,320]{2,1,0:T(8,128)} %fusion.1, bf16[16,320,320]{2,1,0:T(8,128)(2,1)} %all-gather.4.cloned.1.call-done, f32[160,320]{1,0:T(8,128)S(1)} %add.21, f32[160,320]{1,0:T(8,128)S(1)} %collective-permute-done.3), kind=kOutput, calls=%fused_computation.1 | convolution fusion | flops 527718400 | bytes 11878400 | tf_op jit(solution)/shard_map/ac,tcb->tab/dot_general | solution.py:35
  (4 shorter events, 0.1 us)
Async XLA Ops:
  6.5 87.0 %copy-start = (bf16[320,40]{0,1:T(8,128)(2,1)S(1)}, bf16[320,40]{0,1:T(8,128)(2,1)}, u32[]{:S(2)}) copy-start(bf16[320,40]{0,1:T(8,128)(2,1)} %param.10) | copy-start | bytes 76804
  6.5 57.4 %all-gather.6.cloned.1.call-start = ((), (), s32[]{:S(2)}) async-start(), calls=%async_computation.1 | async-start | bytes 5898240 | tf_op jit(solution)/shard_map/all_gather | solution.py:28
  7.3 114.6 %all-gather.4.cloned.1.call-start = ((), (), s32[]{:S(2)}) async-start(), calls=%async_computation | async-start | bytes 5898240 | tf_op jit(solution)/shard_map/all_gather | solution.py:38
  11.1 60.3 %copy-start.3 = (bf16[40,160]{1,0:T(8,128)(2,1)S(1)}, bf16[40,160]{1,0:T(8,128)(2,1)}, u32[]{:S(2)}) copy-start(bf16[40,160]{1,0:T(8,128)(2,1)} %param.11) | copy-start | bytes 38404
  11.1 64.8 %copy-start.2 = (bf16[320,160]{0,1:T(8,128)(2,1)S(1)}, bf16[320,160]{0,1:T(8,128)(2,1)}, u32[]{:S(2)}) copy-start(bf16[320,160]{0,1:T(8,128)(2,1)} %param.9) | copy-start | bytes 307204
  11.1 74.2 %copy-start.1 = (bf16[16,160,320]{2,1,0:T(8,128)(2,1)S(1)}, bf16[16,160,320]{2,1,0:T(8,128)(2,1)}, u32[]{:S(2)}) copy-start(bf16[16,160,320]{2,1,0:T(8,128)(2,1)} %broadcast_select_fusion) | copy-start | bytes 4915204
  68.2 1.6 %collective-permute-start = (f32[160,320]{1,0:T(8,128)S(1)}, f32[160,320]{1,0:T(8,128)S(1)}, u32[]{:S(2)}, u32[]{:S(2)}) collective-permute-start(f32[160,320]{1,0:T(8,128)S(1)} %convolution_bitcast_fusion), channel_id=1, source_target_pairs={{0,2},{2,0},{4,6},{6,4},{8,10},{10,8},{12,14},{14,12},{16,18},{18,... | collective-permute-start | bytes 614408 | tf_op jit(solution)/shard_map/ppermute | solution.py:33
  69.8 14.9 %collective-permute-start.1 = (f32[160,320]{1,0:T(8,128)S(1)}, f32[160,320]{1,0:T(8,128)S(1)}, u32[]{:S(2)}, u32[]{:S(2)}) collective-permute-start(f32[160,320]{1,0:T(8,128)S(1)} %add.19), channel_id=1, source_target_pairs={{0,4},{2,6},{4,0},{6,2},{8,12},{10,14},{12,8},{14,10},{16,20},{18,... | collective-permute-start | bytes 614408 | tf_op jit(solution)/shard_map/ppermute | solution.py:33
  84.7 6.3 %collective-permute-start.2 = (f32[160,320]{1,0:T(8,128)S(1)}, f32[160,320]{1,0:T(8,128)S(1)}, u32[]{:S(2)}, u32[]{:S(2)}) collective-permute-start(f32[160,320]{1,0:T(8,128)S(1)} %add.20), channel_id=1, source_target_pairs={{0,8},{2,10},{4,12},{6,14},{8,0},{10,2},{12,4},{14,6},{16,24},{18,... | collective-permute-start | bytes 614408 | tf_op jit(solution)/shard_map/ppermute | solution.py:33
  91.0 30.9 %collective-permute-start.3 = (f32[160,320]{1,0:T(8,128)S(1)}, f32[160,320]{1,0:T(8,128)S(1)}, u32[]{:S(2)}, u32[]{:S(2)}) collective-permute-start(f32[160,320]{1,0:T(8,128)S(1)} %add.21), channel_id=1, source_target_pairs={{0,16},{2,18},{4,20},{6,22},{8,24},{10,26},{12,28},{14,30},{16,0},... | collective-permute-start | bytes 614408 | tf_op jit(solution)/shard_map/ppermute | solution.py:33
Sparse Core Ops, SparseCore 0:
  8.9 54.9 all-gather.5
  65.4 56.4 all-gather.3
